TPU v7x, 32 devices: a whole 2x2x4 slice. The times are simulated.
32 devices in a mesh: wide: 8 (over y, x, core), narrow: 4 (over z).
Axes of the slice: x: 2, y: 2, z: 4, core: 2. Of those that a mesh axis runs over, the one named last changes fastest.
Arguments:
- loads: bfloat16 [256, 262144], P('narrow', 'wide'), may hold values from -6 to 6
- state: bfloat16 [256, 262144], P('narrow', 'wide'), may hold values from -6 to 6
- modal_diag: float32 [262144], P('wide'), may hold values from 0.5 to 2
- phi: bfloat16 [2048, 128, 128], P('wide'), may hold values from -0.25 to 0.25
- incidence: int32 [2048], P('wide'), may hold values from 0 to 127
- sizes: int32 [1024], P('wide'), may hold values from 1 to 129, as said below
- factor: float32 [16384, 16384], P('wide', 'narrow'), may hold values from -0.046875 to 0.046875
Outputs:
- adjoint: bfloat16 [256, 262144], P('narrow', 'wide')
- sensitivity: float32 [256, 1024], P('narrow', 'wide')
Inputs may be any that keep to these rules, and one draw needn't show every extreme that they name: `sizes`: the 128 substructures of each group hold at most 256 tiles together, and in every draw some group holds exactly 256.
All inputs are finite; a program needn't handle non-finite values.
Results may differ from a plain program's by a relative error of at most 0.015.
Values may be sent and summed in bfloat16 or wider, within the bound.
A program may use at most 128 MiB of HBM per device.

v0:
```python
import functools
import itertools
import jax
import jax.numpy as jnp
from jax import lax
from jax.experimental import pallas as pl
from jax.experimental.pallas import tpu as pltpu
from jax.sharding import PartitionSpec as P

sens_scale = 0.0625
MESH = pl.DeviceIdType.MESH
VMEM_LIMIT = 60 * 1024 * 1024
STEP_TILES = 64


def condense_kernel(tiles, inc_ref, live_ref, loads_ref, phi_ref, out_ref, acc_ref):
    step = pl.program_id(0)
    width = phi_ref.shape[1]

    @pl.when(step == 0)
    def _():
        acc_ref[...] = jnp.zeros_like(acc_ref)

    for j in range(tiles):
        t = step * tiles + j
        term = jnp.dot(
            loads_ref[:, j * width : (j + 1) * width],
            phi_ref[j],
            preferred_element_type=jnp.float32,
        )
        term = jnp.where(t < live_ref[0], term, jnp.zeros_like(term))
        b = inc_ref[t]
        acc_ref[b] = acc_ref[b] + term

    @pl.when(step == pl.num_programs(0) - 1)
    def _():
        out_ref[...] = acc_ref[...].astype(out_ref.dtype)


def recover_kernel(
    tiles, inc_ref, live_ref, loads_ref, state_ref, diag_ref, phi_ref, amp_ref, first_ref, last_ref,
    adj_ref, sens_ref, acc_ref,
):
    step = pl.program_id(0)
    width = phi_ref.shape[1]

    @pl.when(step == 0)
    def _():
        acc_ref[...] = jnp.zeros_like(acc_ref)

    total = acc_ref[...]
    for j in range(tiles):
        t = step * tiles + j
        cols = slice(j * width, (j + 1) * width)
        coupling = lax.dot_general(
            amp_ref[inc_ref[t]], phi_ref[j], (((1,), (1,)), ((), ())),
            preferred_element_type=jnp.float32,
        )
        response = diag_ref[:, cols] * loads_ref[:, cols].astype(jnp.float32) + coupling
        response = jnp.where(t < live_ref[0], response, jnp.zeros_like(response))
        adj_ref[:, cols] = response.astype(adj_ref.dtype)
        row_total = jnp.sum(response * state_ref[:, cols].astype(jnp.float32), axis=1, keepdims=True)
        member = ((first_ref[...] <= t) & (t < last_ref[...])).astype(jnp.float32)
        total = total + row_total * member
    acc_ref[...] = total

    @pl.when(step == pl.num_programs(0) - 1)
    def _():
        sens_ref[...] = acc_ref[...] * sens_scale


def flips_of(index, size):
    bits = [1 << k for k in range(size.bit_length() - 1)]
    raw = [b * (1 - 2 * ((index // b) % 2)) for b in bits]
    low = index % 2
    rest = raw[1:]
    mixed = [rest[k] + low * (rest[-1 - k] - rest[k]) for k in range(len(rest))]
    return raw, raw[:1] + mixed


def combos(count):
    return list(itertools.product((1, 0), repeat=count))


def slot_of(bits, k, c):
    before = sum(1 << (bits - 1 - j) for j in range(k))
    return before + combos(bits - 1 - k).index(c)


def exchange_kernel(wide, narrow, groups, part_ref, factor_ref, out_ref, *scratch):
    (fac, stage, stage_sem, rs_buf, rs_send, rs_recv, chunk, ag_send, ag_recv,
     amp_part, amp_buf, am_send, am_recv, ow_send, ow_recv, work) = scratch[:16]
    per_group = [scratch[16 + 9 * g : 25 + 9 * g] for g in range(len(groups))]
    own_w, own_n = lax.axis_index("wide"), lax.axis_index("narrow")
    _, flips = flips_of(own_w, wide)
    bits = len(flips)
    narrow_raw, _ = flips_of(own_n, narrow)
    peers = [own_n + sum(narrow_raw[b] for b in range(len(narrow_raw)) if i >> b & 1) for i in range(narrow)]
    partners = [own_w + f for f in flips]
    slots, stage_rows, _ = stage.shape
    stages = factor_ref.shape[0] // stage_rows
    load_rows = part_ref.shape[2]
    width = part_ref.shape[3]

    def load(s):
        return pltpu.make_async_copy(
            factor_ref.at[pl.ds(s * stage_rows, stage_rows)], stage.at[s % slots], stage_sem.at[s % slots]
        )

    for s in range(min(slots, stages)):
        load(s).start()

    barrier = pltpu.get_barrier_semaphore()
    for p in partners:
        pl.semaphore_signal(barrier, inc=1, device_id=(p, own_n), device_id_type=MESH)
    for i in range(1, narrow):
        pl.semaphore_signal(barrier, inc=1, device_id=(own_w, peers[i]), device_id_type=MESH)
    pl.semaphore_wait(barrier, bits + narrow - 1)

    sends = []

    def send(src, dst, ssem, rsem, device):
        copy = pltpu.make_async_remote_copy(
            src_ref=src, dst_ref=dst, send_sem=ssem, recv_sem=rsem, device_id=device, device_id_type=MESH
        )
        copy.start()
        sends.append(copy)
        return copy

    def place(k, c):
        return own_w + sum(flips[k + 1 + j] for j in range(len(c)) if c[j])

    def scatter_send(src, buf, ssem, rsem, k, c):
        slot = slot_of(bits, k, c)
        there = slot_of(bits, k, c[::-1]) if k == 0 else slot
        return send(
            src[min(k, 1)].at[place(k, c) + flips[k]], buf.at[there], ssem.at[slot], rsem.at[there],
            (partners[k], own_n),
        )

    def scatter_wait(buf, ssem, rsem, k, slot):
        pltpu.make_async_remote_copy(
            src_ref=buf.at[slot], dst_ref=buf.at[slot], send_sem=ssem.at[slot], recv_sem=rsem.at[slot],
            device_id=(partners[k], own_n), device_id_type=MESH,
        ).wait_recv()

    def scatter_start(src, buf, ssem, rsem):
        return {c: scatter_send(src, buf, ssem, rsem, 0, c) for c in combos(bits - 1)}

    def scatter_step(src, buf, ssem, rsem, pending, k, finish):
        following = {}
        for c in combos(bits - 1 - k):
            slot = slot_of(bits, k, c)
            scatter_wait(buf, ssem, rsem, k, slot)
            d = place(k, c)
            held = src[min(k, 1)]
            total = (held[d].astype(jnp.float32) + buf[slot].astype(jnp.float32)).astype(held.dtype)
            if k == bits - 1:
                finish(total)
            else:
                src[1][d] = total
                if c[0]:
                    following[c[1:]] = scatter_send(src, buf, ssem, rsem, k + 1, c[1:])
        return following

    def gather_send(buf, ssem, rsem, k):
        pending = []
        for c in combos(bits - 1 - k):
            slot = slot_of(bits, k, c)
            d = place(k, c)
            pending.append(send(buf.at[d], buf.at[d], ssem.at[slot], rsem.at[slot], (partners[k], own_n)))
        return pending

    def convert(lo, hi):
        for s in range(lo, hi):
            load(s).wait()
            rows = stage_rows // 8

            def some(r, carry, s=s):
                here = pl.multiple_of(r * rows, rows)
                fac[pl.ds(s * stage_rows + here, rows), :] = stage[s % slots, pl.ds(here, rows), :].astype(fac.dtype)
                return carry

            lax.fori_loop(0, 8, some, 0)
            if s + slots < stages:
                load(s + slots).start()

    def keep_chunk(total):
        chunk[0] = total

    pending = scatter_start((part_ref, work), rs_buf, rs_send, rs_recv)
    for k in range(bits):
        convert(stages * k // (bits + 1), stages * (k + 1) // (bits + 1))
        pending = scatter_step((part_ref, work), rs_buf, rs_send, rs_recv, pending, k, keep_chunk)
    order = [i for group in groups for i in group]
    chunk_copies = {
        i: send(chunk.at[0], chunk.at[i], ag_send.at[i - 1], ag_recv.at[i - 1], (own_w, peers[i]))
        for i in order if i
    }
    convert(stages * bits // (bits + 1), stages)

    state = [None] * len(groups)
    amp_copies = []

    def run(g, stage_index):
        lhs, lhs2, part, p_buf, p_send, p_recv, image, i_send, i_recv = per_group[g]
        group = groups[g]
        if stage_index == 0:
            for a, i in enumerate(group):
                if i:
                    chunk_copies[i].wait_recv()
                for b in range(chunk.shape[1]):
                    lhs[a * load_rows : (a + 1) * load_rows, b * width : (b + 1) * width] = chunk[i, b]
            cols = part.shape[2]

            def one(d, carry):
                here = pl.multiple_of(d * cols, cols)
                part[d] = jnp.dot(
                    lhs[...], fac[:, pl.ds(here, cols)], preferred_element_type=jnp.float32
                ).astype(part.dtype)
                return carry

            lax.fori_loop(0, wide, one, 0)
            state[g] = scatter_start((part, part), p_buf, p_send, p_recv)
        elif stage_index <= bits:
            def keep(total):
                image[own_w] = total

            state[g] = scatter_step((part, part), p_buf, p_send, p_recv, state[g], stage_index - 1, keep)
            if stage_index == bits:
                state[g] = gather_send(image, i_send, i_recv, bits - 1)
        else:
            k = 2 * bits - stage_index
            for copy in state[g]:
                copy.wait_recv()
            if k > 0:
                state[g] = gather_send(image, i_send, i_recv, k - 1)
                return
            cols = image.shape[2]
            for d in range(wide):
                lhs2[:, d * cols : (d + 1) * cols] = image[d]
            rows = 2 * width

            def two(r, carry):
                here = pl.multiple_of(r * rows, rows)
                value = lax.dot_general(
                    lhs2[...], fac[pl.ds(here, rows), :], (((1,), (1,)), ((), ())),
                    preferred_element_type=jnp.float32,
                ).astype(amp_part.dtype)
                for a, i in enumerate(group):
                    for h in range(2):
                        amp_part[i, 2 * r + h] = value[
                            a * load_rows : (a + 1) * load_rows, h * width : (h + 1) * width
                        ]
                return carry

            lax.fori_loop(0, fac.shape[0] // rows, two, 0)
            for i in group:
                if i:
                    amp_copies.append((i, send(
                        amp_part.at[i], amp_buf.at[i - 1], am_send.at[i - 1], am_recv.at[i - 1],
                        (own_w, peers[i]),
                    )))

    last = 2 * bits
    for tick in range(last + len(groups)):
        for g in range(len(groups)):
            if 0 <= tick - g <= last:
                run(g, tick - g)

    total = amp_part[0].astype(jnp.float32)
    for i, copy in amp_copies:
        copy.wait_recv()
        total = total + amp_buf[i - 1].astype(jnp.float32)
    out_ref[own_w] = total.astype(out_ref.dtype)
    for k in range(bits - 1, -1, -1):
        for copy in gather_send(out_ref, ow_send, ow_recv, k):
            copy.wait_recv()
    for copy in sends:
        copy.wait_send()


def exchange(partial, factor, wide, narrow, groups):
    _, blocks, load_rows, width = partial.shape
    own_rows, own_cols = factor.shape
    cols = own_cols // wide
    bf = partial.dtype
    dma = pltpu.SemaphoreType.DMA
    stage_rows = min(128, own_rows)
    scratch = [
        pltpu.VMEM((own_rows, own_cols), bf),
        pltpu.VMEM((4, stage_rows, own_cols), factor.dtype),
        dma((4,)),
        pltpu.VMEM((wide - 1, blocks, load_rows, width), bf), dma((wide - 1,)), dma((wide - 1,)),
        pltpu.VMEM((narrow, blocks, load_rows, width), bf), dma((narrow - 1,)), dma((narrow - 1,)),
        pltpu.VMEM((narrow, blocks, load_rows, width), bf),
        pltpu.VMEM((narrow - 1, blocks, load_rows, width), bf), dma((narrow - 1,)), dma((narrow - 1,)),
        dma((wide - 1,)), dma((wide - 1,)),
        pltpu.VMEM(partial.shape, bf),
    ]
    for group in groups:
        rows = len(group) * load_rows
        scratch += [
            pltpu.VMEM((rows, own_rows), bf), pltpu.VMEM((rows, own_cols), bf),
            pltpu.VMEM((wide, rows, cols), bf),
            pltpu.VMEM((wide - 1, rows, cols), bf), dma((wide - 1,)), dma((wide - 1,)),
            pltpu.VMEM((wide, rows, cols), bf), dma((wide - 1,)), dma((wide - 1,)),
        ]
    return pl.pallas_call(
        functools.partial(exchange_kernel, wide, narrow, groups),
        out_shape=jax.ShapeDtypeStruct(partial.shape, bf),
        in_specs=[pl.BlockSpec(memory_space=pltpu.VMEM), pl.BlockSpec(memory_space=pl.ANY)],
        out_specs=pl.BlockSpec(memory_space=pltpu.VMEM),
        scratch_shapes=scratch,
        compiler_params=pltpu.CompilerParams(
            collective_id=0, has_side_effects=True, vmem_limit_bytes=VMEM_LIMIT
        ),
        name="exchange",
    )(partial, factor)


def groups_of(narrow):
    order = [0] + list(range(narrow - 1, 0, -1))
    size = max(1, narrow // 2)
    return [order[k : k + size] for k in range(0, narrow, size)]


def body(loads, state, modal_diag, phi, incidence, sizes, factor):
    load_cols = loads.shape[0]
    tile_count, width, _ = phi.shape
    subs_local = sizes.shape[0]
    wide, narrow = lax.axis_size("wide"), lax.axis_size("narrow")
    own_blocks = factor.shape[0] // width
    block_count = own_blocks * wide
    running = jnp.cumsum(sizes)
    live = running[-1:]
    tiles = min(STEP_TILES, tile_count)
    steps = tile_count // tiles
    params = pltpu.CompilerParams(dimension_semantics=("arbitrary",), vmem_limit_bytes=VMEM_LIMIT)
    row_spec = pl.BlockSpec((load_cols, tiles * width), lambda s, *_: (0, s))
    phi_spec = pl.BlockSpec((tiles, width, width), lambda s, *_: (s, 0, 0))
    amp_spec = pl.BlockSpec((block_count, load_cols, width), lambda s, *_: (0, 0, 0))
    sub_spec = pl.BlockSpec((1, subs_local), lambda s, *_: (0, 0))
    sens_spec = pl.BlockSpec((load_cols, subs_local), lambda s, *_: (0, 0))

    partial = pl.pallas_call(
        functools.partial(condense_kernel, tiles),
        out_shape=jax.ShapeDtypeStruct((block_count, load_cols, width), jnp.bfloat16),
        grid_spec=pltpu.PrefetchScalarGridSpec(
            num_scalar_prefetch=2, grid=(steps,), in_specs=[row_spec, phi_spec], out_specs=amp_spec,
            scratch_shapes=[pltpu.VMEM((block_count, load_cols, width), jnp.float32)],
        ),
        compiler_params=params,
        name="condense",
    )(incidence, live, loads, phi)
    amp = exchange(
        partial.reshape(wide, own_blocks, load_cols, width), factor, wide, narrow, groups_of(narrow)
    ).reshape(block_count, load_cols, width)
    adjoint, sensitivity = pl.pallas_call(
        functools.partial(recover_kernel, tiles),
        out_shape=(
            jax.ShapeDtypeStruct(loads.shape, jnp.bfloat16),
            jax.ShapeDtypeStruct((load_cols, subs_local), jnp.float32),
        ),
        grid_spec=pltpu.PrefetchScalarGridSpec(
            num_scalar_prefetch=2, grid=(steps,),
            in_specs=[
                row_spec, row_spec, pl.BlockSpec((1, tiles * width), lambda s, *_: (0, s)),
                phi_spec, amp_spec, sub_spec, sub_spec,
            ],
            out_specs=(row_spec, sens_spec),
            scratch_shapes=[pltpu.VMEM((load_cols, subs_local), jnp.float32)],
        ),
        compiler_params=params,
        name="recover",
    )(
        incidence, live, loads, state, modal_diag.reshape(1, -1), phi, amp,
        (running - sizes).reshape(1, -1), running.reshape(1, -1),
    )
    return (adjoint, sensitivity)


def solution(mesh):
    return jax.shard_map(
        body,
        mesh=mesh,
        in_specs=(
            P("narrow", "wide"),
            P("narrow", "wide"),
            P("wide"),
            P("wide", None, None),
            P("wide"),
            P("wide"),
            P("wide", "narrow"),
        ),
        out_specs=(P("narrow", "wide"), P("narrow", "wide")),
        check_vma=False,
    )
```

profile of v0, /device:TPU:0, one launch (start us, length us, event | category | flops | bytes accessed | tf_op | source)
XLA Modules:
  0.0 139.0 jit_solution(3483128073917661)
XLA Ops:
  0.6 0.8 copy.10
  1.4 0.2 reduce-window.4
  1.6 0.5 slice.8
  2.1 0.1 reduce
  2.2 0.0 copy-start
  2.2 1.2 subtract_bitcast_fusion.first_ref
  3.4 9.4 %condense.1 = bf16[128,64,128]{2,1,0:T(8,128)(2,1)} custom-call(s32[256]{0:T(256)} %inc_ref.3, s32[1]{0:T(128)} %bitcast.1.live_ref, bf16[64,32768]{1,0:T(8,128)(2,1)} %loads_ref.3, bf16[256,128,128]{2,1,0:T(8,128)(2,1)} %phi_ref.3), custom_call_target="tpu_custom_call" | custom-call | tf_op jit(solution)/shard_map/condense/pallas_call | solution.py:346
  12.8 0.0 copy-done
  12.8 112.8 %exchange.1 = bf16[8,16,64,128]{3,2,1,0:T(8,128)(2,1)} custom-call(bf16[8,16,64,128]{3,2,1,0:T(8,128)(2,1)} %bitcast.9, f32[2048,4096]{1,0:T(8,128)} %factor_ref.1), custom_call_target="tpu_custom_call" | custom-call | tf_op jit(solution)/shard_map/exchange/pallas_call | solution.py:309
  125.7 13.3 %recover.1 = (bf16[64,32768]{1,0:T(8,128)(2,1)}, f32[64,128]{1,0:T(8,128)}) custom-call(s32[256]{0:T(256)} %inc_ref.3, s32[1]{0:T(128)} %bitcast.1.live_ref, bf16[64,32768]{1,0:T(8,128)(2,1)} %loads_ref.3, bf16[64,32768]{1,0:T(8,128)(2,1)} %state_ref.1, f32[1,32768]{1,0:T(1,128)} %bitcast.10, bf16[256,128,128]{2,1,0:T(8,128)(2,1)} %phi_ref.3, ...), custom_call_target="tpu_custom_call" | custom-call | tf_op jit(solution)/shard_map/recover/pallas_call | solution.py:359
Async XLA Ops:
  2.2 10.7 %copy-start = (s32[128]{0:T(128)}, s32[128]{0:T(128)S(1)}, u32[]{:S(2)}) copy-start(s32[128]{0:T(128)S(1)} %reduce) | copy-start | bytes 1540
where the time goes:
time: 139 us
  Pallas kernels  136 us (98%)
  other arithmetic  1.48 us (1%)
    pallas_call x1, Pallas kernels, exchange(): pl.pallas_call(functools.partial(exchange_kernel, wide, narrow, groups),...  113 us
    pallas_call x1, Pallas kernels, body(): pl.pallas_call(functools.partial(recover_kernel, tiles), out_shape=(jax.S...  13.3 us
    pallas_call x1, Pallas kernels, body(): pl.pallas_call(functools.partial(condense_kernel, tiles), out_shape=jax.S...  9.44 us

commit v1 on v0

v1 whole, which is shorter than its diff:
```python
import functools
import itertools
import jax
import jax.numpy as jnp
from jax import lax
from jax.experimental import pallas as pl
from jax.experimental.pallas import tpu as pltpu
from jax.sharding import PartitionSpec as P

sens_scale = 0.0625
MESH = pl.DeviceIdType.MESH
VMEM_LIMIT = 60 * 1024 * 1024
STEP_TILES = 64


def condense_kernel(tiles, inc_ref, live_ref, loads_ref, phi_ref, out_ref, acc_ref):
    step = pl.program_id(0)
    width = phi_ref.shape[1]

    @pl.when(step == 0)
    def _():
        acc_ref[...] = jnp.zeros_like(acc_ref)

    for j in range(tiles):
        t = step * tiles + j
        term = jnp.dot(
            loads_ref[:, j * width : (j + 1) * width],
            phi_ref[j],
            preferred_element_type=jnp.float32,
        )
        term = jnp.where(t < live_ref[0], term, jnp.zeros_like(term))
        b = inc_ref[t]
        acc_ref[b] = acc_ref[b] + term

    @pl.when(step == pl.num_programs(0) - 1)
    def _():
        chunks, _, rows, _ = out_ref.shape
        for c in range(chunks):
            out_ref[c] = acc_ref[:, c * rows : (c + 1) * rows, :].astype(out_ref.dtype)


def recover_kernel(
    tiles, inc_ref, live_ref, loads_ref, state_ref, diag_ref, phi_ref, amp_ref, first_ref, last_ref,
    adj_ref, sens_ref, acc_ref,
):
    step = pl.program_id(0)
    width = phi_ref.shape[1]

    @pl.when(step == 0)
    def _():
        acc_ref[...] = jnp.zeros_like(acc_ref)

    total = acc_ref[...]
    for j in range(tiles):
        t = step * tiles + j
        cols = slice(j * width, (j + 1) * width)
        b = inc_ref[t]
        amp = jnp.concatenate([amp_ref[c, b] for c in range(amp_ref.shape[0])], axis=0)
        coupling = lax.dot_general(
            amp, phi_ref[j], (((1,), (1,)), ((), ())),
            preferred_element_type=jnp.float32,
        )
        response = diag_ref[:, cols] * loads_ref[:, cols].astype(jnp.float32) + coupling
        response = jnp.where(t < live_ref[0], response, jnp.zeros_like(response))
        adj_ref[:, cols] = response.astype(adj_ref.dtype)
        row_total = jnp.sum(response * state_ref[:, cols].astype(jnp.float32), axis=1, keepdims=True)
        member = ((first_ref[...] <= t) & (t < last_ref[...])).astype(jnp.float32)
        total = total + row_total * member
    acc_ref[...] = total

    @pl.when(step == pl.num_programs(0) - 1)
    def _():
        sens_ref[...] = acc_ref[...] * sens_scale


ORDER = "01C01C01CC001000110110101011"


def chunks_of(load_rows):
    return 2 if load_rows % 32 == 0 else 1


def exchange_kernel(wide, narrow, names, part_ref, factor_ref, out_ref, *scratch):
    ref = dict(zip(names, scratch))
    fac, stage, stage_sem = ref["fac"], ref["stage"], ref["stage_sem"]
    own_w, own_n = lax.axis_index("wide"), lax.axis_index("narrow")
    half = wide // 2
    pair, core = own_w // 2, own_w % 2
    partner = own_w + 1 - 2 * core
    chunks, _, own_blocks, rows, width = part_ref.shape
    total_rows = rows * narrow
    own_rows, own_cols = fac.shape
    cols = own_cols // wide
    pieces = 2
    blocks = own_blocks // pieces
    lines = total_rows // pieces
    bf = part_ref.dtype
    f32 = jnp.float32

    def flipped(index, by, count):
        for k in range(count.bit_length() - 1):
            b = 1 << k
            index = index + ((by // b) % 2) * b * (1 - 2 * ((index // b) % 2))
        return index

    def same(r):
        return 2 * flipped(pair, r, half) + core

    def cross(r):
        return 2 * flipped(pair, r, half) + 1 - core

    peers = [flipped(own_n, i, narrow) for i in range(narrow)]
    far = list(range(half - 1, 0, -1))
    near = list(range(1, half))
    away = list(range(narrow - 1, 0, -1))

    slots, stage_rows, _ = stage.shape
    stages = own_rows // stage_rows

    def load(s):
        return pltpu.make_async_copy(
            factor_ref.at[pl.ds(s * stage_rows, stage_rows)], stage.at[s % slots], stage_sem.at[s % slots]
        )

    for s in range(min(slots, stages)):
        load(s).start()

    barrier = pltpu.get_barrier_semaphore()
    greeted = [(partner, own_n)] + [(cross(r), own_n) for r in far] + [(own_w, peers[i]) for i in away]
    for device in greeted:
        pl.semaphore_signal(barrier, inc=1, device_id=device, device_id_type=MESH)
    pl.semaphore_wait(barrier, len(greeted))

    sends = []

    def send(src, dst, ssem, rsem, device, keep=True):
        pltpu.make_async_remote_copy(
            src_ref=src, dst_ref=dst, send_sem=ssem, recv_sem=rsem, device_id=device, device_id_type=MESH
        ).start()
        if keep:
            sends.append((src, ssem))

    def sent(src, ssem):
        pltpu.make_async_remote_copy(
            src_ref=src, dst_ref=src, send_sem=ssem, recv_sem=ssem, device_id=(partner, own_n), device_id_type=MESH
        ).wait_send()

    def arrived(dst, rsem):
        pltpu.make_async_remote_copy(
            src_ref=dst, dst_ref=dst, send_sem=rsem, recv_sem=rsem, device_id=(partner, own_n), device_id_type=MESH
        ).wait_recv()

    def spread(buf, cut, sems, p):
        own = buf.at[own_w].at[cut(p)]
        xs, xr, ps, pr = sems
        for r in far:
            send(own, own, xs.at[r, p], xr.at[r, p], (cross(r), own_n))
        send(own, own, ps.at[0, p], pr.at[0, p], (partner, own_n))

    def relay(buf, cut, sems, p, r):
        xs, xr, ps, pr = sems
        got = buf.at[cross(r)].at[cut(p)]
        arrived(got, xr.at[r, p])
        send(got, got, ps.at[r, p], pr.at[r, p], (partner, own_n))

    def relayed(buf, cut, sems, p, r):
        slot = same(r) if r else partner
        arrived(buf.at[slot].at[cut(p)], sems[3].at[r, p])

    def block_cut(p):
        return pl.ds(p * blocks, blocks)

    def line_cut(p):
        return pl.ds(p * lines, lines)

    def convert():
        for s in range(stages):
            load(s).wait()
            step = stage_rows // 8

            def some(r, carry, s=s):
                here = pl.multiple_of(r * step, step)
                fac[pl.ds(s * stage_rows + here, step), :] = stage[s % slots, pl.ds(here, step), :].astype(bf)
                return carry

            lax.fori_loop(0, 8, some, 0)
            if s + slots < stages:
                load(s + slots).start()
            if (s + 1) % max(1, stages // 4) == 0:
                yield

    def run(c):
        part = part_ref.at[c]
        c1, c2, cs, held = (ref[k].at[c] for k in ("c1", "c2", "cs", "held"))
        c1s, c1r, c2s, c2r = (ref[k].at[c] for k in ("c1_s", "c1_r", "c2_s", "c2_r"))
        hs, hr = ref["held_s"].at[c], ref["held_r"].at[c]
        for p in range(pieces):
            for r in far:
                send(part.at[same(r), block_cut(p)], c1.at[r, block_cut(p)], c1s.at[r, p], c1r.at[r, p], (partner, own_n))
        for p in range(pieces):
            send(part.at[partner, block_cut(p)], c1.at[0, block_cut(p)], c1s.at[0, p], c1r.at[0, p], (partner, own_n))
        yield
        for p in range(pieces):
            for r in far:
                at = block_cut(p)
                arrived(c1.at[r, at], c1r.at[r, p])
                cs[r - 1, at] = (part[cross(r), at].astype(f32) + c1[r, at].astype(f32)).astype(bf)
                send(cs.at[r - 1, at], c2.at[r - 1, at], c2s.at[r, p], c2r.at[r, p], (cross(r), own_n))
        yield
        for p in range(pieces):
            at = block_cut(p)
            arrived(c1.at[0, at], c1r.at[0, p])
            total = part[own_w, at].astype(f32) + c1[0, at].astype(f32)
            for r in near:
                arrived(c2.at[r - 1, at], c2r.at[r, p])
                total = total + c2[r - 1, at].astype(f32)
            held[0, at] = total.astype(bf)
            for i in away:
                send(held.at[0, at], held.at[i, at], hs.at[i, p], hr.at[i, p], (own_w, peers[i]))
        yield
        lhs = ref["lhs"].at[c]
        for i in range(narrow):
            for p in range(pieces):
                if i:
                    arrived(held.at[i, block_cut(p)], hr.at[i, p])
            for b in range(own_blocks):
                lhs[i * rows : (i + 1) * rows, b * width : (b + 1) * width] = held[i, b]
        i1, i2, isb, given, own_sum, image = (ref[k].at[c] for k in ("i1", "i2", "is", "given", "own_sum", "image"))
        i1s, i1r, i2s, i2r = (ref[k].at[c] for k in ("i1_s", "i1_r", "i2_s", "i2_r"))

        def product(slot):
            here = pl.multiple_of(slot * cols, cols)
            return jnp.dot(lhs[...], fac[:, pl.ds(here, cols)], preferred_element_type=f32)

        def give(j, carry):
            r = half - 1 - j
            other = (r + half - 1) // half
            slot = 2 * flipped(pair, r, half) + core * other + (1 - core) * (1 - other)
            given[r] = product(slot).astype(bf)
            for p in range(pieces):
                at = line_cut(p)
                send(given.at[r, at], i1.at[r, at], i1s.at[r, p], i1r.at[r, p], (partner, own_n), keep=False)
            return carry

        lax.fori_loop(0, half, give, 0)

        def keep(j, carry):
            r = half - 1 - j
            value = product(cross(r))
            for p in range(pieces):
                arrived(i1.at[r, line_cut(p)], i1r.at[r, p])
            isb[r - 1] = (value + i1[r].astype(f32)).astype(bf)
            for p in range(pieces):
                at = line_cut(p)
                send(isb.at[r - 1, at], i2.at[r - 1, at], i2s.at[r, p], i2r.at[r, p], (cross(r), own_n), keep=False)
            return carry

        lax.fori_loop(0, half - 1, keep, 0)
        for p in range(pieces):
            at = line_cut(p)
            sends.extend((given.at[r, at], i1s.at[r, p]) for r in range(half))
            sends.extend((isb.at[r - 1, at], i2s.at[r, p]) for r in near)
        own_sum[...] = product(own_w)
        yield
        im = tuple(ref["im" + k].at[c] for k in ("_xs", "_xr", "_ps", "_pr"))
        for p in range(pieces):
            at = line_cut(p)
            arrived(i1.at[0, at], i1r.at[0, p])
            total = own_sum[at] + i1[0, at].astype(f32)
            for r in near:
                arrived(i2.at[r - 1, at], i2r.at[r, p])
                total = total + i2[r - 1, at].astype(f32)
            image[own_w, at] = total.astype(bf)
            spread(image, line_cut, im, p)
        yield
        acc, amp, amp_in = ref["acc"].at[c], ref["amp"].at[c], ref["amp_in"].at[c]
        as_, ar = ref["amp_s"].at[c], ref["amp_r"].at[c]
        tile = min(4 * width, own_rows // pieces)
        tiles = own_rows // tile

        def contract(q, first, last, t):
            here = pl.multiple_of(t * tile, tile)
            there = pl.multiple_of(2 * q * cols, 2 * cols)
            left = jnp.concatenate([image[2 * q], image[2 * q + 1]], axis=1)
            value = lax.dot_general(
                left, fac[pl.ds(here, tile), pl.ds(there, 2 * cols)], (((1,), (1,)), ((), ())),
                preferred_element_type=f32,
            )
            if not first:
                value = value + acc[:, pl.ds(here, tile)]
            if not last:
                acc[:, pl.ds(here, tile)] = value
                return
            value = value.astype(bf)
            for i in range(narrow):
                for h in range(tile // width):
                    amp[i, t * (tile // width) + h] = value[i * rows : (i + 1) * rows, h * width : (h + 1) * width]

        def contract_some(q, first, last, lo, hi):
            def one(t, carry):
                contract(q, first, last, t)
                return carry

            lax.fori_loop(lo, hi, one, 0)

        for p in range(pieces):
            relayed(image, line_cut, im, p, 0)
        contract_some(pair, True, half == 1, 0, tiles)
        yield
        for p in range(pieces):
            for r in near:
                relay(image, line_cut, im, p, r)
        yield
        for r in near[:-1]:
            for p in range(pieces):
                relayed(image, line_cut, im, p, r)
            contract_some(flipped(pair, r, half), False, False, 0, tiles)
        for r in near[-1:]:
            for p in range(pieces):
                relayed(image, line_cut, im, p, r)
            for p in range(pieces):
                contract_some(flipped(pair, r, half), False, True, tiles * p // pieces, tiles * (p + 1) // pieces)
                at = block_cut(p)
                for i in away:
                    send(amp.at[i, at], amp_in.at[i - 1, at], as_.at[i, p], ar.at[i, p], (own_w, peers[i]))
        yield
        out = out_ref.at[c]
        om = tuple(ref["out" + k].at[c] for k in ("_xs", "_xr", "_ps", "_pr"))
        for p in range(pieces):
            at = block_cut(p)
            total = amp[0, at].astype(f32)
            for i in away[::-1]:
                arrived(amp_in.at[i - 1, at], ar.at[i, p])
                total = total + amp_in[i - 1, at].astype(f32)
            out[own_w, at] = total.astype(bf)
            spread(out, block_cut, om, p)
        yield
        for p in range(pieces):
            for r in near:
                relay(out, block_cut, om, p, r)
        yield
        for p in range(pieces):
            for r in [0] + near:
                relayed(out, block_cut, om, p, r)

    runs = {str(c): run(c) for c in range(chunks)}
    runs["C"] = convert()
    for who in ORDER:
        if who in runs:
            next(runs[who], None)
    for gen in runs.values():
        for _ in gen:
            pass
    for src, ssem in sends:
        sent(src, ssem)


def exchange(partial, factor, wide, narrow):
    chunks, _, own_blocks, rows, width = partial.shape
    own_rows, own_cols = factor.shape
    cols = own_cols // wide
    half = wide // 2
    total_rows = rows * narrow
    bf, f32 = partial.dtype, jnp.float32
    dma = pltpu.SemaphoreType.DMA
    pieces = 2
    stage_rows = min(128, own_rows)
    slot = (own_blocks, rows, width)
    strip = (total_rows, cols)
    spec = {
        "fac": pltpu.VMEM((own_rows, own_cols), bf),
        "stage": pltpu.VMEM((4, stage_rows, own_cols), factor.dtype),
        "stage_sem": dma((4,)),
        "c1": pltpu.VMEM((chunks, half) + slot, bf),
        "c2": pltpu.VMEM((chunks, half - 1) + slot, bf),
        "cs": pltpu.VMEM((chunks, half - 1) + slot, bf),
        "held": pltpu.VMEM((chunks, narrow) + slot, bf),
        "lhs": pltpu.VMEM((chunks, total_rows, own_rows), bf),
        "i1": pltpu.VMEM((chunks, half) + strip, bf),
        "i2": pltpu.VMEM((chunks, half - 1) + strip, bf),
        "is": pltpu.VMEM((chunks, half - 1) + strip, bf),
        "given": pltpu.VMEM((chunks, half) + strip, bf),
        "own_sum": pltpu.VMEM((chunks,) + strip, f32),
        "image": pltpu.VMEM((chunks, wide) + strip, bf),
        "acc": pltpu.VMEM((chunks, total_rows, own_rows), f32),
        "amp": pltpu.VMEM((chunks, narrow) + slot, bf),
        "amp_in": pltpu.VMEM((chunks, narrow - 1) + slot, bf),
    }
    for k in ("c1_s", "c1_r", "c2_s", "c2_r", "i1_s", "i1_r", "i2_s", "i2_r"):
        spec[k] = dma((chunks, half, pieces))
    for k in ("held_s", "held_r", "amp_s", "amp_r"):
        spec[k] = dma((chunks, narrow, pieces))
    for a in ("im", "out"):
        for k in ("_xs", "_xr", "_ps", "_pr"):
            spec[a + k] = dma((chunks, half, pieces))
    return pl.pallas_call(
        functools.partial(exchange_kernel, wide, narrow, tuple(spec)),
        out_shape=jax.ShapeDtypeStruct(partial.shape, bf),
        in_specs=[pl.BlockSpec(memory_space=pltpu.VMEM), pl.BlockSpec(memory_space=pl.ANY)],
        out_specs=pl.BlockSpec(memory_space=pltpu.VMEM),
        scratch_shapes=list(spec.values()),
        compiler_params=pltpu.CompilerParams(
            collective_id=0, has_side_effects=True, vmem_limit_bytes=VMEM_LIMIT
        ),
        name="exchange",
    )(partial, factor)


def body(loads, state, modal_diag, phi, incidence, sizes, factor):
    load_cols = loads.shape[0]
    tile_count, width, _ = phi.shape
    subs_local = sizes.shape[0]
    wide, narrow = lax.axis_size("wide"), lax.axis_size("narrow")
    own_blocks = factor.shape[0] // width
    block_count = own_blocks * wide
    running = jnp.cumsum(sizes)
    live = running[-1:]
    tiles = min(STEP_TILES, tile_count)
    steps = tile_count // tiles
    params = pltpu.CompilerParams(dimension_semantics=("arbitrary",), vmem_limit_bytes=VMEM_LIMIT)
    row_spec = pl.BlockSpec((load_cols, tiles * width), lambda s, *_: (0, s))
    phi_spec = pl.BlockSpec((tiles, width, width), lambda s, *_: (s, 0, 0))
    chunks = chunks_of(load_cols)
    chunk_shape = (chunks, block_count, load_cols // chunks, width)
    amp_spec = pl.BlockSpec(chunk_shape, lambda s, *_: (0, 0, 0, 0))
    sub_spec = pl.BlockSpec((1, subs_local), lambda s, *_: (0, 0))
    sens_spec = pl.BlockSpec((load_cols, subs_local), lambda s, *_: (0, 0))

    partial = pl.pallas_call(
        functools.partial(condense_kernel, tiles),
        out_shape=jax.ShapeDtypeStruct(chunk_shape, jnp.bfloat16),
        grid_spec=pltpu.PrefetchScalarGridSpec(
            num_scalar_prefetch=2, grid=(steps,), in_specs=[row_spec, phi_spec], out_specs=amp_spec,
            scratch_shapes=[pltpu.VMEM((block_count, load_cols, width), jnp.float32)],
        ),
        compiler_params=params,
        name="condense",
    )(incidence, live, loads, phi)
    amp = exchange(
        partial.reshape(chunks, wide, own_blocks, load_cols // chunks, width), factor, wide, narrow
    ).reshape(chunk_shape)
    adjoint, sensitivity = pl.pallas_call(
        functools.partial(recover_kernel, tiles),
        out_shape=(
            jax.ShapeDtypeStruct(loads.shape, jnp.bfloat16),
            jax.ShapeDtypeStruct((load_cols, subs_local), jnp.float32),
        ),
        grid_spec=pltpu.PrefetchScalarGridSpec(
            num_scalar_prefetch=2, grid=(steps,),
            in_specs=[
                row_spec, row_spec, pl.BlockSpec((1, tiles * width), lambda s, *_: (0, s)),
                phi_spec, amp_spec, sub_spec, sub_spec,
            ],
            out_specs=(row_spec, sens_spec),
            scratch_shapes=[pltpu.VMEM((load_cols, subs_local), jnp.float32)],
        ),
        compiler_params=params,
        name="recover",
    )(
        incidence, live, loads, state, modal_diag.reshape(1, -1), phi, amp,
        (running - sizes).reshape(1, -1), running.reshape(1, -1),
    )
    return (adjoint, sensitivity)


def solution(mesh):
    return jax.shard_map(
        body,
        mesh=mesh,
        in_specs=(
            P("narrow", "wide"),
            P("narrow", "wide"),
            P("wide"),
            P("wide", None, None),
            P("wide"),
            P("wide"),
            P("wide", "narrow"),
        ),
        out_specs=(P("narrow", "wide"), P("narrow", "wide")),
        check_vma=False,
    )
```

time: 139 us -> 122 us (0.88)
  Pallas kernels: 136 us -> 118 us
    pallas_call x1, Pallas kernels: 113 us -> 95.2 us  [exchange(): pl.pallas_call(functools.partial(exchange_kernel, wide, narrow, tuple(spe...]
where the time goes in v1:
time: 122 us; the launch traced here: 121 us
  Pallas kernels  118 us (97%)
  other arithmetic  1.48 us (1%)
  local copies, waits for them, and re-layouts  1.29 us (1%)
    pallas_call x1, Pallas kernels, exchange(): pl.pallas_call(functools.partial(exchange_kernel, wide, narrow, tuple(spe...  95.2 us
    pallas_call x1, Pallas kernels, body(): pl.pallas_call(functools.partial(recover_kernel, tiles), out_shape=(jax.S...  13.4 us
    pallas_call x1, Pallas kernels, body(): pl.pallas_call(functools.partial(condense_kernel, tiles), out_shape=jax.S...  9.44 us

profile of v1, /device:TPU:0, one launch (start us, length us, event | category | flops | bytes accessed | tf_op | source)
XLA Modules:
  0.0 121.5 jit_solution(7338957070059619880)
XLA Ops:
  0.6 0.8 copy.10
  1.4 0.2 reduce-window.4
  1.6 0.5 slice.8
  2.1 0.1 reduce
  2.2 0.0 copy-start
  2.2 1.2 subtract_bitcast_fusion.first_ref
  3.4 9.4 %condense.1 = bf16[2,128,32,128]{3,2,1,0:T(8,128)(2,1)} custom-call(s32[256]{0:T(256)} %inc_ref.3, s32[1]{0:T(128)} %bitcast.1.live_ref, bf16[64,32768]{1,0:T(8,128)(2,1)} %loads_ref.3, bf16[256,128,128]{2,1,0:T(8,128)(2,1)} %phi_ref.3), custom_call_target="tpu_custom_call" | custom-call | tf_op jit(solution)/shard_map/condense/pallas_call | solution.py:429
  12.8 0.0 copy-done
  12.8 95.2 %exchange.1 = bf16[2,8,16,32,128]{4,3,2,1,0:T(8,128)(2,1)} custom-call(bf16[2,8,16,32,128]{4,3,2,1,0:T(8,128)(2,1)} %bitcast.9, f32[2048,4096]{1,0:T(8,128)} %factor_ref.1), custom_call_target="tpu_custom_call" | custom-call | tf_op jit(solution)/shard_map/exchange/pallas_call | solution.py:396
  108.1 13.4 %recover.1 = (bf16[64,32768]{1,0:T(8,128)(2,1)}, f32[64,128]{1,0:T(8,128)}) custom-call(s32[256]{0:T(256)} %inc_ref.3, s32[1]{0:T(128)} %bitcast.1.live_ref, bf16[64,32768]{1,0:T(8,128)(2,1)} %loads_ref.3, bf16[64,32768]{1,0:T(8,128)(2,1)} %state_ref.1, f32[1,32768]{1,0:T(1,128)} %bitcast.10, bf16[256,128,128]{2,1,0:T(8,128)(2,1)} %phi_ref.3, ...), custom_call_target="tpu_custom_call" | custom-call | tf_op jit(solution)/shard_map/recover/pallas_call | solution.py:442
Async XLA Ops:
  2.2 10.7 %copy-start = (s32[128]{0:T(128)}, s32[128]{0:T(128)S(1)}, u32[]{:S(2)}) copy-start(s32[128]{0:T(128)S(1)} %reduce) | copy-start | bytes 1540
